TPU v7x, 256 devices: a whole 4x4x8 slice. The times are simulated.
256 devices in a mesh: dp: 32 (over z, y_lo, core), space: 8 (over x, y_hi).
Axes of the slice: x: 4, y: 4 (y_hi: 2, y_lo: 2; y = y_hi * 2 + y_lo), z: 8, core: 2. Of those that a mesh axis runs over, the one named last changes fastest.
Arguments:
- occupancy: int32 [32, 5, 128, 128], P('dp', None, 'space'), may hold values from 0 to 8191
- state_labels: int32 [32, 8, 8], P('dp', 'space'), may hold values 0 or 1
- lift_weight: bfloat16 [13, 32], replicated, may hold values from -1.75 to 1.75
- temporal_weight: bfloat16 [3, 3, 5, 32, 64], replicated, may hold values from -0.21875 to 0.21875
- middle_weight: bfloat16 [3, 3, 64, 128], replicated, may hold values from -0.375 to 0.375
- deeper_weight: bfloat16 [3, 3, 128, 256], replicated, may hold values from -0.25 to 0.25
- deepest_weight: bfloat16 [3, 3, 256, 512], replicated, may hold values from -0.1875 to 0.1875
- head_weight: bfloat16 [512], replicated, may hold values from -0.25 to 0.25
Outputs:
- temporal_grad: float32 [3, 3, 5, 32, 64], replicated
- middle_grad: float32 [3, 3, 64, 128], replicated
- deeper_grad: float32 [3, 3, 128, 256], replicated
- deepest_grad: float32 [3, 3, 256, 512], replicated
- head_grad: float32 [512], replicated
All inputs are finite; a program needn't handle non-finite values. No bound on the sum of `state_labels` on one device may be relied on, other than what follows from the above.
Results may differ from a plain program's by a relative error of at most 0.015.
Values may be sent and summed in bfloat16 or wider, within the bound.
A program may use at most 64 MiB of HBM per device.

v0:
```python
import jax
import jax.numpy as jnp
from jax import lax
from jax.sharding import PartitionSpec as P


def from_behind(block, axis, distance):
    devices = range(lax.axis_size(axis))
    route = [(i - distance, i) for i in devices if i - distance in devices]
    return lax.ppermute(block, axis, route)


def conv_layer(feature_map, weight):
    upper_row = from_behind(feature_map[:, :, -1:, :], "space", 1)
    padded = jnp.concatenate([upper_row, feature_map], axis=2)
    padded = jnp.pad(padded, ((0, 0), (0, 0), (0, 0), (1, 0)))
    accumulated = lax.conv_general_dilated(
        padded,
        weight,
        (2, 2),
        "VALID",
        dimension_numbers=("NCHW", "HWIO", "NCHW"),
        preferred_element_type=jnp.float32,
    )
    gate = jax.nn.sigmoid(accumulated)
    slope = gate * (1.0 + accumulated * (1.0 - gate))
    return ((accumulated * gate).astype(jnp.bfloat16), slope, padded)


def weight_grad(padded, delta):
    return lax.conv_general_dilated(
        padded,
        delta,
        (1, 1),
        "VALID",
        rhs_dilation=(2, 2),
        dimension_numbers=("CNHW", "IOHW", "HWNC"),
        preferred_element_type=jnp.float32,
    )


def input_grad(delta, weight):
    flipped = weight[::-1, ::-1]
    accumulated = lax.conv_general_dilated(
        delta,
        flipped,
        (1, 1),
        ((2, 2), (2, 2)),
        lhs_dilation=(2, 2),
        dimension_numbers=("NCHW", "HWOI", "NCHW"),
        preferred_element_type=jnp.float32,
    )
    lower_row = from_behind(accumulated[:, :, 0:1, 1:], "space", -1)
    local_part = accumulated[:, :, 1:, 1:]
    return jnp.concatenate([local_part[:, :, :-1], local_part[:, :, -1:] + lower_row], axis=2)


def local(
    occupancy,
    state_labels,
    lift_weight,
    temporal_weight,
    middle_weight,
    deeper_weight,
    deepest_weight,
    head_weight,
):
    samples_here = occupancy.shape[0]
    frames = occupancy.shape[1]
    heights = lift_weight.shape[0]
    lift_width = lift_weight.shape[1]
    shifts = jnp.arange(heights, dtype=jnp.int32)
    height_bits = jnp.bitwise_and(
        jnp.right_shift(occupancy[:, :, None], shifts[None, None, :, None, None]), 1
    ).astype(jnp.bfloat16)
    lifted = jnp.einsum(
        "stcrw,ck->stkrw", height_bits, lift_weight, preferred_element_type=jnp.float32
    )
    lifted = jnp.maximum(lifted, 0.0).astype(jnp.bfloat16)
    lifted = lifted.reshape(samples_here, frames * lift_width, lifted.shape[3], lifted.shape[4])
    first_kernel = temporal_weight.reshape(3, 3, frames * lift_width, temporal_weight.shape[4])
    first_map, first_slope, lifted_padded = conv_layer(lifted, first_kernel)
    second_map, second_slope, first_padded = conv_layer(first_map, middle_weight)
    third_map, third_slope, second_padded = conv_layer(second_map, deeper_weight)
    fourth_map, fourth_slope, third_padded = conv_layer(third_map, deepest_weight)
    batch_total = state_labels.shape[0] * lax.axis_size("dp")
    logits = jnp.einsum("sorw,o->srw", fourth_map, head_weight, preferred_element_type=jnp.float32)
    logit_grad = (jax.nn.sigmoid(logits) - state_labels.astype(jnp.float32)) / batch_total
    head_float = head_weight.astype(jnp.float32)
    head_grad = jnp.einsum("sorw,srw->o", fourth_map.astype(jnp.float32), logit_grad)
    fourth_delta = (logit_grad[:, None] * head_float[None, :, None, None] * fourth_slope).astype(
        jnp.bfloat16
    )
    deepest_grad = weight_grad(third_padded, fourth_delta)
    third_delta = (input_grad(fourth_delta, deepest_weight) * third_slope).astype(jnp.bfloat16)
    deeper_grad = weight_grad(second_padded, third_delta)
    second_delta = (input_grad(third_delta, deeper_weight) * second_slope).astype(jnp.bfloat16)
    middle_grad = weight_grad(first_padded, second_delta)
    first_delta = (input_grad(second_delta, middle_weight) * first_slope).astype(jnp.bfloat16)
    temporal_grad = weight_grad(lifted_padded, first_delta).reshape(temporal_weight.shape)
    reduced = lax.psum(
        (temporal_grad, middle_grad, deeper_grad, deepest_grad, head_grad), ("dp", "space")
    )
    return (reduced[0], reduced[1], reduced[2], reduced[3], reduced[4])


def solution(mesh):
    return jax.shard_map(
        local,
        mesh=mesh,
        in_specs=(
            P("dp", None, "space", None),
            P("dp", "space", None),
            P(),
            P(),
            P(),
            P(),
            P(),
            P(),
        ),
        out_specs=(P(), P(), P(), P(), P()),
        check_vma=False,
    )
```

profile of v0, /device:TPU:8, one launch (start us, length us, event | category | flops | bytes accessed | tf_op | source)
XLA Modules:
  0.0 403.2 jit_solution(4823248896462357719)
XLA Ops:
  8.8 2.8 copy.146
  12.7 4.2 %collective-permute-start = (bf16[1,160,1,128]{1,0,3,2:T(2,128)(2,1)S(1)}, bf16[1,160,1,128]{1,0,3,2:T(2,128)(2,1)S(1)}, u32[]{:S(2)}, u32[]{:S(2)}) collective-permute-start(bf16[1,160,1,128]{1,0,3,2:T(2,128)(2,1)S(1)} %slice.81), channel_id=1, source_target_pairs={{0,1},{1,2},{2,3},{3,4},{4,5},{5,6},{6,7},{8,9},{9,10},{10,11},{11... | collective-permute-start | bytes 122888 | tf_op jit(solution)/shard_map/ppermute | solution.py:10
  16.9 2.7 collective-permute-done
  19.6 6.2 %pad_maximum_fusion = bf16[1,160,17,128]{1,0,3,2:T(2,128)(2,1)} fusion(bf16[1,160,16,128]{1,0,3,2:T(2,128)(2,1)} %copy.146, bf16[1,160,1,128]{1,0,3,2:T(2,128)(2,1)S(1)} %collective-permute-done), kind=kLoop, calls=%fused_computation.2 | loop fusion | flops 348160 | bytes 1392640 | tf_op jit(solution)/shard_map/concatenate | solution.py:15
  25.9 5.9 %copy.148 = bf16[1,160,17,128]{3,1,2,0:T(8,128)(2,1)} copy(bf16[1,160,17,128]{1,0,3,2:T(2,128)(2,1)} %pad_maximum_fusion) | data formatting | bytes 1392640 | tf_op jit(solution)/shard_map/concatenate | solution.py:15
  31.8 1.7 copy.200
  35.0 3.4 reshape.106
  38.4 1.8 copy.151
  40.2 1.6 add_multiply_fusion
  41.9 5.9 %collective-permute-start.1 = (bf16[1,64,1,64]{1,0,3,2:T(2,128)(2,1)S(1)}, bf16[1,64,1,64]{1,0,3,2:T(2,128)(2,1)S(1)}, u32[]{:S(2)}, u32[]{:S(2)}) collective-permute-start(bf16[1,64,1,64]{1,0,3,2:T(2,128)(2,1)S(1)} %slice_bitcast_fusion.1), channel_id=1, source_target_pairs={{0,1},{1,2},{2,3},{3,4},{4,5},{5,6},{6,7},{8,9},{9,10},{10,11},{11... | collective-permute-start | bytes 24584 | tf_op jit(solution)/shard_map/ppermute | solution.py:10
  50.4 1.9 add_multiply_fusion.1
  52.4 5.7 %collective-permute-start.2 = (bf16[1,128,1,32]{1,0,3,2:T(2,128)(2,1)S(1)}, bf16[1,128,1,32]{1,0,3,2:T(2,128)(2,1)S(1)}, u32[]{:S(2)}, u32[]{:S(2)}) collective-permute-start(bf16[1,128,1,32]{1,0,3,2:T(2,128)(2,1)S(1)} %slice_bitcast_fusion.3), channel_id=1, source_target_pairs={{0,1},{1,2},{2,3},{3,4},{4,5},{5,6},{6,7},{8,9},{9,10},{10,11},{11... | collective-permute-start | bytes 24584 | tf_op jit(solution)/shard_map/ppermute | solution.py:10
  60.6 5.9 %collective-permute-start.3 = (bf16[1,256,1,16]{1,0,3,2:T(2,128)(2,1)S(1)}, bf16[1,256,1,16]{1,0,3,2:T(2,128)(2,1)S(1)}, u32[]{:S(2)}, u32[]{:S(2)}) collective-permute-start(bf16[1,256,1,16]{1,0,3,2:T(2,128)(2,1)S(1)} %slice_bitcast_fusion.2), channel_id=1, source_target_pairs={{0,1},{1,2},{2,3},{3,4},{4,5},{5,6},{6,7},{8,9},{9,10},{10,11},{11... | collective-permute-start | bytes 24584 | tf_op jit(solution)/shard_map/ppermute | solution.py:10
  72.2 3.1 fusion.62
  75.2 3.8 collective-permute-done.4
  82.5 5.2 %collective-permute-done.5 = f32[1,128,1,32]{1,0,3,2:T(1,128)S(1)} collective-permute-done((f32[1,128,1,32]{1,0,3,2:T(1,128)S(1)}, f32[1,128,1,32]{1,0,3,2:T(1,128)S(1)}, u32[]{:S(2)}, u32[]{:S(2)}) %collective-permute-start.5) | collective-permute-done | bytes 16416 | tf_op jit(solution)/shard_map/ppermute | solution.py:10
  89.9 2.5 fusion.93
  92.4 4.4 %collective-permute-done.6 = f32[1,64,1,64]{1,3,2,0:T(8,128)S(1)} collective-permute-done((f32[1,64,1,64]{1,3,2,0:T(8,128)S(1)}, f32[1,64,1,64]{1,3,2,0:T(8,128)S(1)}, u32[]{:S(2)}, u32[]{:S(2)}) %collective-permute-start.6) | collective-permute-done | bytes 16416 | tf_op jit(solution)/shard_map/ppermute | solution.py:10
  96.9 5.6 %fusion.25 = f32[3,3,160,64]{3,2,1,0:T(8,128)} fusion(bf16[1,160,17,128]{1,0,3,2:T(2,128)(2,1)S(1)} %copy-done.1, bf16[1,64,8,64]{1,3,2,0:T(8,128)(2,1)S(1)} %fusion.24), kind=kOutput, calls=%fused_computation.40 | convolution fusion | flops 93880320 | bytes 1130496 | tf_op jit(solution)/shard_map/conv_general_dilated | solution.py:31
  103.3 80.2 %psum.39 = f32[512]{0:T(512)} all-reduce(f32[512]{0:T(512)S(1)} %bitcast.187), channel_id=1, replica_groups=mesh['dp'=32,'space'=8] {'dp','space'}, use_global_device_ids=true, to_apply=%region_4.5 | all-reduce | flops 512 | bytes 4096 | tf_op jit(solution)/shard_map/psum | solution.py:101
  183.5 202.9 %all-reduce.3.cloned.1.call-done = (f32[3,3,5,32,64]{4,3,2,1,0:T(8,128)}, f32[3,3,64,128]{3,2,1,0:T(8,128)}, f32[3,3,128,256]{3,2,1,0:T(8,128)}, f32[3,3,256,512]{3,2,1,0:T(8,128)}) async-done(((f32[3,3,5,32,64]{4,3,2,1,0:T(8,128)}, f32[3,3,64,128]{3,2,1,0:T(8,128)}, f32[3,3,128,256]{3,2,1,0:T(8,128)}, f32[3,3,256,512]{3,2,1,0:T(8,128)}), (f32[3,3,5,32,64]{4,3,2,1,0:T(8,128)}, f32[3,3,64,128]{3,2,1,0:T(8,128)}, ...) | async-done | bytes 6561808 | tf_op jit(solution)/shard_map/psum | solution.py:101
  386.4 2.1 copy.241
  388.6 1.7 copy.242
  391.3 5.0 %copy.244 = f32[3,3,256,512]{3,2,1,0:T(8,128)} copy(f32[3,3,256,512]{3,2,1,0:T(8,128)} %get-tuple-element.22) | data formatting | bytes 9437184
  (133 shorter events, 22.1 us)
Async XLA Ops:
  7.2 61.5 %copy-start = (bf16[3,3,256,512]{3,2,1,0:T(8,128)(2,1)S(1)}, bf16[3,3,256,512]{3,2,1,0:T(8,128)(2,1)}, u32[]{:S(2)}) copy-start(bf16[3,3,256,512]{3,2,1,0:T(8,128)(2,1)} %param.14) | copy-start | bytes 7077892
  7.2 379.3 %all-reduce.3.cloned.1.call-start = ((), (), s32[]{:S(2)}) async-start(), calls=%async_computation | async-start | bytes 13860864 | tf_op jit(solution)/shard_map/psum | solution.py:101
  12.7 6.9 %collective-permute-start = (bf16[1,160,1,128]{1,0,3,2:T(2,128)(2,1)S(1)}, bf16[1,160,1,128]{1,0,3,2:T(2,128)(2,1)S(1)}, u32[]{:S(2)}, u32[]{:S(2)}) collective-permute-start(bf16[1,160,1,128]{1,0,3,2:T(2,128)(2,1)S(1)} %slice.81), channel_id=1, source_target_pairs={{0,1},{1,2},{2,3},{3,4},{4,5},{5,6},{6,7},{8,9},{9,10},{10,11},{11... | collective-permute-start | bytes 122888 | tf_op jit(solution)/shard_map/ppermute | solution.py:10
  38.3 1.8 copy-start.15
  38.3 1.8 copy-start.17
  41.8 8.6 %copy-start.18 = (pred[8,5]{0,1:T(8,128)(4,1)S(1)}, pred[8,5]{0,1:T(8,128)(4,1)}, u32[]{:S(2)}) copy-start(pred[8,5]{0,1:T(8,128)(4,1)} %constant.40) | copy-start | bytes 124
  41.9 7.5 %collective-permute-start.1 = (bf16[1,64,1,64]{1,0,3,2:T(2,128)(2,1)S(1)}, bf16[1,64,1,64]{1,0,3,2:T(2,128)(2,1)S(1)}, u32[]{:S(2)}, u32[]{:S(2)}) collective-permute-start(bf16[1,64,1,64]{1,0,3,2:T(2,128)(2,1)S(1)} %slice_bitcast_fusion.1), channel_id=1, source_target_pairs={{0,1},{1,2},{2,3},{3,4},{4,5},{5,6},{6,7},{8,9},{9,10},{10,11},{11... | collective-permute-start | bytes 24584 | tf_op jit(solution)/shard_map/ppermute | solution.py:10
  49.8 10.7 %copy-start.3 = (bf16[1,64,9,64]{1,0,3,2:T(2,128)(2,1)}, bf16[1,64,9,64]{1,0,3,2:T(2,128)(2,1)S(1)}, u32[]{:S(2)}) copy-start(bf16[1,64,9,64]{1,0,3,2:T(2,128)(2,1)S(1)} %pad_maximum_fusion.1) | copy-start | bytes 221188
  49.8 10.4 %copy-start.19 = (pred[8,3]{0,1:T(4,128)(4,1)S(1)}, pred[8,3]{0,1:T(4,128)(4,1)}, u32[]{:S(2)}) copy-start(pred[8,3]{0,1:T(4,128)(4,1)} %constant.39) | copy-start | bytes 76
  50.2 16.3 %copy-start.10 = (bf16[512]{0:T(512)(128)(2,1)S(1)}, bf16[512]{0:T(512)(128)(2,1)}, u32[]{:S(2)}) copy-start(bf16[512]{0:T(512)(128)(2,1)} %param.15) | copy-start | bytes 3076
  50.3 9.9 %copy-start.5 = (bf16[3,3,128,256]{3,2,1,0:T(8,128)(2,1)S(1)}, bf16[3,3,128,256]{3,2,1,0:T(8,128)(2,1)}, u32[]{:S(2)}) copy-start(bf16[3,3,128,256]{3,2,1,0:T(8,128)(2,1)} %param.13) | copy-start | bytes 1769476
  52.3 16.3 %copy-start.14 = (pred[8,2]{0,1:T(4,128)(4,1)S(1)}, pred[8,2]{0,1:T(4,128)(4,1)}, u32[]{:S(2)}) copy-start(pred[8,2]{0,1:T(4,128)(4,1)} %constant.38) | copy-start | bytes 52
  52.4 7.2 %collective-permute-start.2 = (bf16[1,128,1,32]{1,0,3,2:T(2,128)(2,1)S(1)}, bf16[1,128,1,32]{1,0,3,2:T(2,128)(2,1)S(1)}, u32[]{:S(2)}, u32[]{:S(2)}) collective-permute-start(bf16[1,128,1,32]{1,0,3,2:T(2,128)(2,1)S(1)} %slice_bitcast_fusion.3), channel_id=1, source_target_pairs={{0,1},{1,2},{2,3},{3,4},{4,5},{5,6},{6,7},{8,9},{9,10},{10,11},{11... | collective-permute-start | bytes 24584 | tf_op jit(solution)/shard_map/ppermute | solution.py:10
  60.1 8.1 %copy-start.7 = (f32[4,8,5,128]{3,1,2,0:T(8,128)S(1)}, f32[4,8,5,128]{3,1,2,0:T(8,128)}, u32[]{:S(2)}) copy-start(f32[4,8,5,128]{3,1,2,0:T(8,128)} %get-tuple-element.11) | copy-start | bytes 245764
  60.6 7.9 %collective-permute-start.3 = (bf16[1,256,1,16]{1,0,3,2:T(2,128)(2,1)S(1)}, bf16[1,256,1,16]{1,0,3,2:T(2,128)(2,1)S(1)}, u32[]{:S(2)}, u32[]{:S(2)}) collective-permute-start(bf16[1,256,1,16]{1,0,3,2:T(2,128)(2,1)S(1)} %slice_bitcast_fusion.2), channel_id=1, source_target_pairs={{0,1},{1,2},{2,3},{3,4},{4,5},{5,6},{6,7},{8,9},{9,10},{10,11},{11... | collective-permute-start | bytes 24584 | tf_op jit(solution)/shard_map/ppermute | solution.py:10
  70.7 10.3 %copy-start.9 = (bf16[1,128,1,32]{1,0,3,2:T(2,128)(2,1)S(1)}, bf16[1,128,1,32]{1,0,3,2:T(2,128)(2,1)}, u32[]{:S(2)}) copy-start(bf16[1,128,1,32]{1,0,3,2:T(2,128)(2,1)} %copy-done.8) | copy-start | bytes 24580
  70.7 8.3 %collective-permute-start.4 = (f32[1,256,1,16]{1,0,3,2:T(1,128)S(1)}, f32[1,256,1,16]{1,0,3,2:T(1,128)S(1)}, u32[]{:S(2)}, u32[]{:S(2)}) collective-permute-start(f32[1,256,1,16]{1,0,3,2:T(1,128)S(1)} %get-tuple-element.14), channel_id=1, source_target_pairs={{1,0},{2,1},{3,2},{4,3},{5,4},{6,5},{7,6},{9,8},{10,9},{11,10},{12... | collective-permute-start | bytes 49160 | tf_op jit(solution)/shard_map/ppermute | solution.py:10
  79.5 8.4 %copy-start.6 = (bf16[3,3,64,128]{3,2,1,0:T(8,128)(2,1)S(1)}, bf16[3,3,64,128]{3,2,1,0:T(8,128)(2,1)}, u32[]{:S(2)}) copy-start(bf16[3,3,64,128]{3,2,1,0:T(8,128)(2,1)} %param.12) | copy-start | bytes 442372
  79.5 8.4 %copy-start.11 = (pred[8,10]{0,1:T(8,128)(4,1)S(1)}, pred[8,10]{0,1:T(8,128)(4,1)}, u32[]{:S(2)}) copy-start(pred[8,10]{0,1:T(8,128)(4,1)} %constant.37) | copy-start | bytes 244
  79.5 8.2 %collective-permute-start.5 = (f32[1,128,1,32]{1,0,3,2:T(1,128)S(1)}, f32[1,128,1,32]{1,0,3,2:T(1,128)S(1)}, u32[]{:S(2)}, u32[]{:S(2)}) collective-permute-start(f32[1,128,1,32]{1,0,3,2:T(1,128)S(1)} %slice.103), channel_id=1, source_target_pairs={{1,0},{2,1},{3,2},{4,3},{5,4},{6,5},{7,6},{9,8},{10,9},{11,10},{12... | collective-permute-start | bytes 49160 | tf_op jit(solution)/shard_map/ppermute | solution.py:10
  88.5 8.4 %copy-start.4 = (f32[8,1,64,64]{3,0,2,1:T(8,128)S(1)}, f32[8,1,64,64]{3,0,2,1:T(8,128)}, u32[]{:S(2)}) copy-start(f32[8,1,64,64]{3,0,2,1:T(8,128)} %slice.110) | copy-start | bytes 393220
  88.5 8.4 %copy-start.1 = (bf16[1,160,17,128]{1,0,3,2:T(2,128)(2,1)S(1)}, bf16[1,160,17,128]{1,0,3,2:T(2,128)(2,1)}, u32[]{:S(2)}) copy-start(bf16[1,160,17,128]{1,0,3,2:T(2,128)(2,1)} %pad_maximum_fusion) | copy-start | bytes 2088964
  88.5 8.3 %collective-permute-start.6 = (f32[1,64,1,64]{1,3,2,0:T(8,128)S(1)}, f32[1,64,1,64]{1,3,2,0:T(8,128)S(1)}, u32[]{:S(2)}, u32[]{:S(2)}) collective-permute-start(f32[1,64,1,64]{1,3,2,0:T(8,128)S(1)} %slice.109), channel_id=1, source_target_pairs={{1,0},{2,1},{3,2},{4,3},{5,4},{6,5},{7,6},{9,8},{10,9},{11,10},{12... | collective-permute-start | bytes 49160 | tf_op jit(solution)/shard_map/ppermute | solution.py:10
  386.4 3.8 copy-start.2
  (4 other events, 3.4 us)
Sparse Core Ops, SparseCore 0:
  102.7 283.7 all-reduce.2
where the time goes:
time: 404 us; the launch traced here: 403 us
  waiting for transfers between devices  222 us (55%)
  blocking collectives  80.2 us (20%)
  local copies, waits for them, and re-layouts  33.2 us (8%)
  starting transfers between devices  26 us (6%)
  matrix products  20 us (5%)
  between operations  14.8 us (4%)
  other arithmetic  7.19 us (2%)
    psum x1, waiting for transfers between devices, local(): lax.psum((temporal_grad, middle_grad, deeper_grad, deepest_grad, head_gra...  203 us
    psum x1, blocking collectives, local(): lax.psum((temporal_grad, middle_grad, deeper_grad, deepest_grad, head_gra...  80.2 us
    ppermute x7, starting transfers between devices, from_behind(): return lax.ppermute(block, axis, route)  26 us
    ppermute x7, waiting for transfers between devices, from_behind(): return lax.ppermute(block, axis, route)  18.8 us
    unnamed x54, local copies, waits for them, and re-layouts  13.6 us
    conv_general_dilated x4, matrix products, weight_grad(): lax.conv_general_dilated(padded, delta, (1, 1), 'VALID', rhs_dilation=(2,...  12.7 us
  transfers between devices with their start and end apart: 8, of which 7 were waited for; matrix products, arithmetic and copies ran while one was open for 2% of the time, Pallas kernels for 0%

commit v1 on v0

--- a/solution.py
+++ b/solution.py
@@ -99,7 +99,7 @@
     first_delta = (input_grad(second_delta, middle_weight) * first_slope).astype(jnp.bfloat16)
     temporal_grad = weight_grad(lifted_padded, first_delta).reshape(temporal_weight.shape)
     reduced = lax.psum(
-        (temporal_grad, middle_grad, deeper_grad, deepest_grad, head_grad), ("dp", "space")
+        lax.psum((temporal_grad, middle_grad, deeper_grad, deepest_grad, head_grad), "dp"), "space"
     )
     return (reduced[0], reduced[1], reduced[2], reduced[3], reduced[4])
 

time: 404 us -> 677 us (1.68)
  waiting for transfers between devices: 222 us -> 463 us
  blocking collectives: 80.2 us -> 106 us
    psum x0 -> x1, waiting for transfers between devices: none -> 194 us  [local(): lax.psum(lax.psum((temporal_grad, middle_grad, deeper_grad, deepest_grad,...]
    psum x1, waiting for transfers between devices: 203 us -> 251 us  [local(): lax.psum((temporal_grad, middle_grad, deeper_grad, deepest_grad, head_gra...]
    psum x0 -> x1, blocking collectives: none -> 38.5 us  [local(): lax.psum(lax.psum((temporal_grad, middle_grad, deeper_grad, deepest_grad,...]
    psum x1, blocking collectives: 80.2 us -> 67 us  [local(): lax.psum((temporal_grad, middle_grad, deeper_grad, deepest_grad, head_gra...]
  transfers between devices with their start and end apart: 8 -> 9, of which waited for: 7 -> 8; matrix products, arithmetic and copies ran while one was open for 2% -> 1% of each run, Pallas kernels for 0% -> 0%
where the time goes in v1:
time: 677 us; the launch traced here: 670 us
  waiting for transfers between devices  463 us (68%)
  blocking collectives  106 us (16%)
  local copies, waits for them, and re-layouts  33.2 us (5%)
  starting transfers between devices  26.1 us (4%)
  matrix products  20 us (3%)
  between operations  14.8 us (2%)
  other arithmetic  7.2 us (1%)
    psum x1, waiting for transfers between devices, local(): lax.psum((temporal_grad, middle_grad, deeper_grad, deepest_grad, head_gra...  251 us
    psum x1, waiting for transfers between devices, local(): lax.psum(lax.psum((temporal_grad, middle_grad, deeper_grad, deepest_grad,...  194 us
    psum x1, blocking collectives, local(): lax.psum((temporal_grad, middle_grad, deeper_grad, deepest_grad, head_gra...  67 us
    psum x1, blocking collectives, local(): lax.psum(lax.psum((temporal_grad, middle_grad, deeper_grad, deepest_grad,...  38.5 us
    ppermute x7, starting transfers between devices, from_behind(): return lax.ppermute(block, axis, route)  26 us
    ppermute x7, waiting for transfers between devices, from_behind(): return lax.ppermute(block, axis, route)  18.8 us
    unnamed x54, local copies, waits for them, and re-layouts  13.6 us
  transfers between devices with their start and end apart: 9, of which 8 were waited for; matrix products, arithmetic and copies ran while one was open for 1% of the time, Pallas kernels for 0%

profile of v1, /device:TPU:8, one launch (start us, length us, event | category | flops | bytes accessed | tf_op | source)
XLA Modules:
  0.0 669.8 jit_solution(14238176099312989811)
XLA Ops:
  8.8 2.8 copy.146
  12.7 4.2 collective-permute-start
  16.9 2.7 collective-permute-done
  19.6 6.2 pad_maximum_fusion
  25.9 5.9 copy.148
  35.0 3.4 reshape.106
  38.4 1.8 copy.151
  41.9 5.9 collective-permute-start.1
  50.4 1.9 add_multiply_fusion.1
  52.4 5.7 collective-permute-start.2
  60.6 5.9 collective-permute-start.3
  72.2 3.1 fusion.62
  75.2 3.8 collective-permute-done.4
  82.5 5.2 collective-permute-done.5
  89.9 2.5 fusion.93
  92.4 4.4 collective-permute-done.6
  96.9 5.6 fusion.25
  102.6 250.5 %all-reduce.5.cloned.1.call-done = (f32[3,3,5,32,64]{4,3,2,1,0:T(8,128)}, f32[3,3,64,128]{3,2,1,0:T(8,128)}, f32[3,3,128,256]{3,2,1,0:T(8,128)}, f32[3,3,256,512]{3,2,1,0:T(8,128)}) async-done(((f32[3,3,5,32,64]{4,3,2,1,0:T(8,128)}, f32[3,3,64,128]{3,2,1,0:T(8,128)}, f32[3,3,128,256]{3,2,1,0:T(8,128)}, f32[3,3,256,512]{3,2,1,0:T(8,128)}), (f32[3,3,5,32,64]{4,3,2,1,0:T(8,128)}, f32[3,3,64,128]{3,2,1,0:T(8,128)}, ...) | async-done | bytes 6561808 | tf_op jit(solution)/shard_map/psum | solution.py:102
  353.9 67.0 %psum.78 = f32[512]{0:T(512)S(1)} all-reduce(f32[512]{0:T(512)S(1)} %bitcast.187), channel_id=1, replica_groups=mesh['dp'=32,'space'=8] {'dp'}, use_global_device_ids=true, to_apply=%region_8.9 | all-reduce | flops 512 | bytes 4096 | tf_op jit(solution)/shard_map/psum | solution.py:102
  421.0 38.5 %psum.79 = f32[512]{0:T(512)} all-reduce(f32[512]{0:T(512)S(1)} %psum.78), channel_id=1, replica_groups=mesh['dp'=32,'space'=8] {'space'}, use_global_device_ids=true, to_apply=%region_9.10 | all-reduce | flops 512 | bytes 4096 | tf_op jit(solution)/shard_map/psum | solution.py:101
  459.5 193.6 %all-reduce.7.cloned.1.call-done = (f32[3,3,5,32,64]{4,3,2,1,0:T(8,128)}, f32[3,3,64,128]{3,2,1,0:T(8,128)}, f32[3,3,128,256]{3,2,1,0:T(8,128)}, f32[3,3,256,512]{3,2,1,0:T(8,128)}) async-done(((f32[3,3,5,32,64]{4,3,2,1,0:T(8,128)}, f32[3,3,64,128]{3,2,1,0:T(8,128)}, f32[3,3,128,256]{3,2,1,0:T(8,128)}, f32[3,3,256,512]{3,2,1,0:T(8,128)}), (f32[3,3,5,32,64]{4,3,2,1,0:T(8,128)}, f32[3,3,64,128]{3,2,1,0:T(8,128)}, ...) | async-done | bytes 6561808 | tf_op jit(solution)/shard_map/psum | solution.py:101
  653.1 2.1 copy.245
  655.2 1.7 copy.246
  657.9 5.0 copy.248
  (137 shorter events, 25.4 us)
Async XLA Ops:
  7.2 61.5 %copy-start = (bf16[3,3,256,512]{3,2,1,0:T(8,128)(2,1)S(1)}, bf16[3,3,256,512]{3,2,1,0:T(8,128)(2,1)}, u32[]{:S(2)}) copy-start(bf16[3,3,256,512]{3,2,1,0:T(8,128)(2,1)} %param.14) | copy-start | bytes 7077892
  7.2 346.0 %all-reduce.5.cloned.1.call-start = ((), (), s32[]{:S(2)}) async-start(), calls=%async_computation | async-start | bytes 13860864 | tf_op jit(solution)/shard_map/psum | solution.py:102
  12.7 6.9 %collective-permute-start = (bf16[1,160,1,128]{1,0,3,2:T(2,128)(2,1)S(1)}, bf16[1,160,1,128]{1,0,3,2:T(2,128)(2,1)S(1)}, u32[]{:S(2)}, u32[]{:S(2)}) collective-permute-start(bf16[1,160,1,128]{1,0,3,2:T(2,128)(2,1)S(1)} %slice.81), channel_id=1, source_target_pairs={{0,1},{1,2},{2,3},{3,4},{4,5},{5,6},{6,7},{8,9},{9,10},{10,11},{11... | collective-permute-start | bytes 122888 | tf_op jit(solution)/shard_map/ppermute | solution.py:10
  38.4 1.8 copy-start.17
  41.8 8.6 %copy-start.18 = (pred[8,5]{0,1:T(8,128)(4,1)S(1)}, pred[8,5]{0,1:T(8,128)(4,1)}, u32[]{:S(2)}) copy-start(pred[8,5]{0,1:T(8,128)(4,1)} %constant.40) | copy-start | bytes 124
  41.9 7.5 %collective-permute-start.1 = (bf16[1,64,1,64]{1,0,3,2:T(2,128)(2,1)S(1)}, bf16[1,64,1,64]{1,0,3,2:T(2,128)(2,1)S(1)}, u32[]{:S(2)}, u32[]{:S(2)}) collective-permute-start(bf16[1,64,1,64]{1,0,3,2:T(2,128)(2,1)S(1)} %slice_bitcast_fusion.1), channel_id=1, source_target_pairs={{0,1},{1,2},{2,3},{3,4},{4,5},{5,6},{6,7},{8,9},{9,10},{10,11},{11... | collective-permute-start | bytes 24584 | tf_op jit(solution)/shard_map/ppermute | solution.py:10
  49.8 10.7 %copy-start.3 = (bf16[1,64,9,64]{1,0,3,2:T(2,128)(2,1)}, bf16[1,64,9,64]{1,0,3,2:T(2,128)(2,1)S(1)}, u32[]{:S(2)}) copy-start(bf16[1,64,9,64]{1,0,3,2:T(2,128)(2,1)S(1)} %pad_maximum_fusion.1) | copy-start | bytes 221188
  49.8 10.4 %copy-start.19 = (pred[8,3]{0,1:T(4,128)(4,1)S(1)}, pred[8,3]{0,1:T(4,128)(4,1)}, u32[]{:S(2)}) copy-start(pred[8,3]{0,1:T(4,128)(4,1)} %constant.39) | copy-start | bytes 76
  50.2 16.3 %copy-start.10 = (bf16[512]{0:T(512)(128)(2,1)S(1)}, bf16[512]{0:T(512)(128)(2,1)}, u32[]{:S(2)}) copy-start(bf16[512]{0:T(512)(128)(2,1)} %param.15) | copy-start | bytes 3076
  50.3 9.9 %copy-start.5 = (bf16[3,3,128,256]{3,2,1,0:T(8,128)(2,1)S(1)}, bf16[3,3,128,256]{3,2,1,0:T(8,128)(2,1)}, u32[]{:S(2)}) copy-start(bf16[3,3,128,256]{3,2,1,0:T(8,128)(2,1)} %param.13) | copy-start | bytes 1769476
  52.3 16.3 %copy-start.14 = (pred[8,2]{0,1:T(4,128)(4,1)S(1)}, pred[8,2]{0,1:T(4,128)(4,1)}, u32[]{:S(2)}) copy-start(pred[8,2]{0,1:T(4,128)(4,1)} %constant.38) | copy-start | bytes 52
  52.4 7.2 %collective-permute-start.2 = (bf16[1,128,1,32]{1,0,3,2:T(2,128)(2,1)S(1)}, bf16[1,128,1,32]{1,0,3,2:T(2,128)(2,1)S(1)}, u32[]{:S(2)}, u32[]{:S(2)}) collective-permute-start(bf16[1,128,1,32]{1,0,3,2:T(2,128)(2,1)S(1)} %slice_bitcast_fusion.3), channel_id=1, source_target_pairs={{0,1},{1,2},{2,3},{3,4},{4,5},{5,6},{6,7},{8,9},{9,10},{10,11},{11... | collective-permute-start | bytes 24584 | tf_op jit(solution)/shard_map/ppermute | solution.py:10
  60.2 8.1 %copy-start.7 = (f32[4,8,5,128]{3,1,2,0:T(8,128)S(1)}, f32[4,8,5,128]{3,1,2,0:T(8,128)}, u32[]{:S(2)}) copy-start(f32[4,8,5,128]{3,1,2,0:T(8,128)} %get-tuple-element.15) | copy-start | bytes 245764
  60.6 7.9 %collective-permute-start.3 = (bf16[1,256,1,16]{1,0,3,2:T(2,128)(2,1)S(1)}, bf16[1,256,1,16]{1,0,3,2:T(2,128)(2,1)S(1)}, u32[]{:S(2)}, u32[]{:S(2)}) collective-permute-start(bf16[1,256,1,16]{1,0,3,2:T(2,128)(2,1)S(1)} %slice_bitcast_fusion.2), channel_id=1, source_target_pairs={{0,1},{1,2},{2,3},{3,4},{4,5},{5,6},{6,7},{8,9},{9,10},{10,11},{11... | collective-permute-start | bytes 24584 | tf_op jit(solution)/shard_map/ppermute | solution.py:10
  70.7 10.3 %copy-start.9 = (bf16[1,128,1,32]{1,0,3,2:T(2,128)(2,1)S(1)}, bf16[1,128,1,32]{1,0,3,2:T(2,128)(2,1)}, u32[]{:S(2)}) copy-start(bf16[1,128,1,32]{1,0,3,2:T(2,128)(2,1)} %copy-done.8) | copy-start | bytes 24580
  70.7 8.3 %collective-permute-start.4 = (f32[1,256,1,16]{1,0,3,2:T(1,128)S(1)}, f32[1,256,1,16]{1,0,3,2:T(1,128)S(1)}, u32[]{:S(2)}, u32[]{:S(2)}) collective-permute-start(f32[1,256,1,16]{1,0,3,2:T(1,128)S(1)} %get-tuple-element.18), channel_id=1, source_target_pairs={{1,0},{2,1},{3,2},{4,3},{5,4},{6,5},{7,6},{9,8},{10,9},{11,10},{12... | collective-permute-start | bytes 49160 | tf_op jit(solution)/shard_map/ppermute | solution.py:10
  79.5 8.4 %copy-start.6 = (bf16[3,3,64,128]{3,2,1,0:T(8,128)(2,1)S(1)}, bf16[3,3,64,128]{3,2,1,0:T(8,128)(2,1)}, u32[]{:S(2)}) copy-start(bf16[3,3,64,128]{3,2,1,0:T(8,128)(2,1)} %param.12) | copy-start | bytes 442372
  79.5 8.4 %copy-start.11 = (pred[8,10]{0,1:T(8,128)(4,1)S(1)}, pred[8,10]{0,1:T(8,128)(4,1)}, u32[]{:S(2)}) copy-start(pred[8,10]{0,1:T(8,128)(4,1)} %constant.37) | copy-start | bytes 244
  79.5 8.2 %collective-permute-start.5 = (f32[1,128,1,32]{1,0,3,2:T(1,128)S(1)}, f32[1,128,1,32]{1,0,3,2:T(1,128)S(1)}, u32[]{:S(2)}, u32[]{:S(2)}) collective-permute-start(f32[1,128,1,32]{1,0,3,2:T(1,128)S(1)} %slice.103), channel_id=1, source_target_pairs={{1,0},{2,1},{3,2},{4,3},{5,4},{6,5},{7,6},{9,8},{10,9},{11,10},{12... | collective-permute-start | bytes 49160 | tf_op jit(solution)/shard_map/ppermute | solution.py:10
  88.5 8.4 %copy-start.4 = (f32[8,1,64,64]{3,0,2,1:T(8,128)S(1)}, f32[8,1,64,64]{3,0,2,1:T(8,128)}, u32[]{:S(2)}) copy-start(f32[8,1,64,64]{3,0,2,1:T(8,128)} %slice.110) | copy-start | bytes 393220
  88.5 8.4 %copy-start.1 = (bf16[1,160,17,128]{1,0,3,2:T(2,128)(2,1)S(1)}, bf16[1,160,17,128]{1,0,3,2:T(2,128)(2,1)}, u32[]{:S(2)}) copy-start(bf16[1,160,17,128]{1,0,3,2:T(2,128)(2,1)} %pad_maximum_fusion) | copy-start | bytes 2088964
  88.5 8.3 %collective-permute-start.6 = (f32[1,64,1,64]{1,3,2,0:T(8,128)S(1)}, f32[1,64,1,64]{1,3,2,0:T(8,128)S(1)}, u32[]{:S(2)}, u32[]{:S(2)}) collective-permute-start(f32[1,64,1,64]{1,3,2,0:T(8,128)S(1)} %slice.109), channel_id=1, source_target_pairs={{1,0},{2,1},{3,2},{4,3},{5,4},{6,5},{7,6},{9,8},{10,9},{11,10},{12... | collective-permute-start | bytes 49160 | tf_op jit(solution)/shard_map/ppermute | solution.py:10
  102.6 550.5 %all-reduce.7.cloned.1.call-start = ((), (), s32[]{:S(2)}) async-start(), calls=%async_computation.1 | async-start | bytes 13860864 | tf_op jit(solution)/shard_map/psum | solution.py:101
  653.1 3.8 copy-start.2
  (5 other events, 5.3 us)
Sparse Core Ops, SparseCore 0:
  102.7 250.4 all-reduce.4
  356.1 296.9 all-reduce.6
